TPU v7x, 32 devices: a whole 2x2x4 slice. The times are simulated.
32 devices in a mesh: cohort: 2 (over x), grp: 4 (over z), vox: 4 (over y, core).
Axes of the slice: x: 2, y: 2, z: 4, core: 2. Of those that a mesh axis runs over, the one named last changes fastest.
Arguments:
- probes: bfloat16 [16384, 256], P(('cohort', 'grp', 'vox')), parts along dimension 0, may hold values from -6 to 6
- blocks: bfloat16 [512, 4, 128, 128], P(('cohort', 'grp', 'vox')), parts along dimension 0, may hold values from -0.25 to 0.25
- pattern: int32 [512, 4], P(('cohort', 'grp', 'vox')), parts along dimension 0, may hold values from 0 to 31, as said below
- scale_exp: int32 [512, 4], P(('cohort', 'grp', 'vox')), parts along dimension 0, may hold values from -2 to 2
- noise: float32 [512, 128], P(('cohort', 'grp', 'vox')), parts along dimension 0, may hold values from 0.1 to 1
Outputs:
- hessian_probes: float32 [16384, 256], P(('cohort', 'grp', 'vox')), parts along dimension 0
There are 2 independent parts, one for each index of `cohort`. A program takes and returns all parts, laid end to end along the dimension named above; each array names one. Nothing has to cross between parts.
Inputs may be any that keep to these rules, and one draw needn't show every extreme that they name: pattern is below 16 in the last group's rows; other rows may reach into the next group's parameter blocks.
All inputs are finite; a program needn't handle non-finite values.
Results may differ from a plain program's by a relative error of at most 0.0016.
Values may be sent and summed in bfloat16 or wider, within the bound.
No kernel may reach another device: no remote copies, remote signals or barrier semaphores. Data moves between devices by JAX's collectives and lax.ppermute only.
A program may use at most 128 MiB of HBM per device.

v0:
```python
import jax
import jax.numpy as jnp
from jax import lax
from jax.sharding import PartitionSpec as P


def shifted(array, axis, by):
    devices = lax.axis_size(axis)
    pairs = [(i, i + by) for i in range(devices) if 0 <= i + by < devices]
    return lax.ppermute(array, axis, pairs)


def local(probes, blocks, pattern, scale_exp, noise):
    rows_here = blocks.shape[0]
    width = blocks.shape[2]
    count = blocks.shape[1]
    probe_cols = probes.shape[1]
    own_panel = lax.all_gather(probes, "vox", axis=0, tiled=True)
    next_rows = shifted(own_panel, "grp", -1)
    group_rows = own_panel.shape[0] // width
    panels = jnp.concatenate([own_panel, next_rows], axis=0).reshape(
        2 * group_rows, width, probe_cols
    )
    scales = jnp.exp2(scale_exp.astype(jnp.float32))
    forward = jnp.zeros((rows_here, width, probe_cols), jnp.float32)
    for slot in range(count):
        picked = panels[pattern[:, slot]]
        product = jnp.einsum(
            "rab,rbk->rak", blocks[:, slot], picked, preferred_element_type=jnp.float32
        )
        forward = forward + product * scales[:, slot, None, None]
    weighted = (noise[:, :, None] * forward).astype(jnp.bfloat16)
    partial_value = jnp.zeros((2 * group_rows, width, probe_cols), jnp.float32)
    for slot in range(count):
        back = jnp.einsum(
            "rab,rak->rbk", blocks[:, slot], weighted, preferred_element_type=jnp.float32
        )
        partial_value = partial_value.at[pattern[:, slot]].add(back * scales[:, slot, None, None])
    own_part = partial_value[:group_rows].reshape(group_rows * width, probe_cols)
    next_part = partial_value[group_rows:].reshape(group_rows * width, probe_cols)
    mine, theirs = (
        lax.psum_scatter(own_part, "vox", scatter_dimension=0, tiled=True),
        lax.psum_scatter(next_part, "vox", scatter_dimension=0, tiled=True),
    )
    result = mine + shifted(theirs, "grp", 1)
    return result


def solution(mesh):
    in_specs = (
        P(("cohort", "grp", "vox"), None),
        P(("cohort", "grp", "vox"), None, None, None),
        P(("cohort", "grp", "vox"), None),
        P(("cohort", "grp", "vox"), None),
        P(("cohort", "grp", "vox"), None),
    )
    out_specs = P(("cohort", "grp", "vox"), None)
    return jax.shard_map(local, mesh=mesh, in_specs=in_specs, out_specs=out_specs, check_vma=False)
```

profile of v0, /device:TPU:0, one launch (start us, length us, event | category | flops | bytes accessed | tf_op | source)
XLA Modules:
  0.0 187.7 jit_solution(3924717938640009242)
XLA Ops:
  6.5 0.7 all-gather.2.cloned.1.call-update
  7.3 21.0 %all-gather.2.cloned.1.call-done = bf16[2048,256]{1,0:T(8,128)(2,1)} async-done(((bf16[512,256]{1,0:T(8,128)(2,1)}), bf16[2048,256]{1,0:T(8,128)(2,1)}) %all-gather.2.cloned.1.call-update) | async-done | bytes 1048592 | tf_op jit(solution)/shard_map/all_gather | solution.py:18
  28.3 1.3 collective-permute-start
  29.6 0.8 fusion.22
  30.5 0.7 multiply_exponential_fusion
  31.2 24.5 %collective-permute-done = bf16[2048,256]{1,0:T(8,128)(2,1)S(1)} collective-permute-done((bf16[2048,256]{1,0:T(8,128)(2,1)}, bf16[2048,256]{1,0:T(8,128)(2,1)S(1)}, u32[]{:S(2)}, u32[]{:S(2)}) %collective-permute-start) | collective-permute-done | bytes 1048608 | tf_op jit(solution)/shard_map/ppermute | solution.py:10
  55.7 1.4 pad_maximum_fusion
  57.1 0.6 gather_fusion.2
  57.7 1.6 gather_fusion.1
  59.3 3.0 %fusion.3 = f32[16,256,128]{2,1,0:T(8,128)} fusion(bf16[16,128,256]{2,1,0:T(8,128)(2,1)S(1)} %gather_fusion.2, bf16[16,4,128,128]{3,2,1,0:T(8,128)(2,1)} %param.6), kind=kOutput, calls=%fused_computation.17 | convolution fusion | flops 134217728 | bytes 3670016 | tf_op jit(solution)/shard_map/rab,rbk->rak/dot_general | solution.py:28
  62.3 2.8 %fusion.6 = f32[16,256,128]{2,1,0:T(8,128)} fusion(bf16[16,128,256]{2,1,0:T(8,128)(2,1)S(1)} %copy-done.2, bf16[16,4,128,128]{3,2,1,0:T(8,128)(2,1)} %param.6), kind=kOutput, calls=%fused_computation.20 | convolution fusion | flops 134217728 | bytes 3670016 | tf_op jit(solution)/shard_map/rab,rbk->rak/dot_general | solution.py:28
  65.1 0.6 gather_fusion
  65.8 2.8 %fusion.9 = f32[16,256,128]{2,1,0:T(8,128)} fusion(bf16[16,128,256]{2,1,0:T(8,128)(2,1)S(1)} %gather_fusion, bf16[16,4,128,128]{3,2,1,0:T(8,128)(2,1)} %param.6), kind=kOutput, calls=%fused_computation.23 | convolution fusion | flops 134217728 | bytes 3670016 | tf_op jit(solution)/shard_map/rab,rbk->rak/dot_general | solution.py:28
  69.3 4.2 %multiply_convert_fusion = bf16[16,256,128]{2,1,0:T(8,128)(2,1)S(1)} fusion(f32[16,256,128]{2,1,0:T(8,128)} %fusion.3, f32[16,256,128]{2,1,0:T(8,128)} %fusion.6, f32[16,256,128]{2,1,0:T(8,128)} %fusion.9, bf16[16,128,256]{2,1,0:T(8,128)(2,1)S(1)} %gather_fusion.3, f32[16,128]{1,0:T(8,128)S(1)} %copy-done.3, f32[16]{0:T(128)S(1)} %get-tuple-element.8, ...), kind=kOutput, calls=%fused_computation.9 | convolution fusion | flops 138936320 | bytes 8921344 | tf_op jit(solution)/shard_map/rab,rbk->rak/dot_general | solution.py:28
  73.9 1.7 multiply_bitcast_fusion.2
  75.6 1.8 multiply_bitcast_fusion.1
  77.4 1.8 multiply_bitcast_fusion
  79.2 1.9 copy.22
  81.0 3.1 %copy.23 = f32[16,128,256]{2,1,0:T(8,128)} copy(f32[16,128,256]{1,2,0:T(8,128)} %multiply_bitcast_fusion.2) | data formatting | bytes 4194304 | tf_op jit(solution)/shard_map/mul | solution.py:38
  84.1 1.8 copy.24
  85.9 1.9 %copy.25 = f32[16,128,256]{2,1,0:T(8,128)S(1)} copy(f32[16,128,256]{1,2,0:T(8,128)} %multiply_bitcast_fusion) | data formatting | bytes 4194304 | tf_op jit(solution)/shard_map/mul | solution.py:38
  87.9 2.4 %broadcast_in_dim.2 = f32[32,128,256]{2,1,0:T(8,128)} broadcast(f32[]{:T(128)} %constant.0.clone.1), dimensions={} | broadcast | bytes 4194308 | tf_op jit(solution)/shard_map/broadcast_in_dim | solution.py:33
  90.3 5.3 %scatter_fusion = f32[32,128,256]{2,1,0:T(8,128)} fusion(f32[32,128,256]{2,1,0:T(8,128)} %broadcast_in_dim.2, s32[16]{0:T(128)S(1)} %get-tuple-element.13, f32[16,128,256]{2,1,0:T(8,128)} %copy.22), kind=kCustom, calls=%fused_computation.4 | custom fusion | flops 524288 | bytes 6291520 | tf_op jit(solution)/shard_map/scatter-add | solution.py:38
  95.5 5.2 %scatter_fusion.1 = f32[32,128,256]{2,1,0:T(8,128)} fusion(f32[32,128,256]{2,1,0:T(8,128)} %scatter_fusion, s32[16]{0:T(128)S(1)} %get-tuple-element.12, f32[16,128,256]{2,1,0:T(8,128)} %copy.23), kind=kCustom, calls=%fused_computation.5 | custom fusion | flops 524288 | bytes 6291520 | tf_op jit(solution)/shard_map/scatter-add | solution.py:38
  100.7 5.2 %scatter_fusion.2 = f32[32,128,256]{2,1,0:T(8,128)} fusion(f32[32,128,256]{2,1,0:T(8,128)} %scatter_fusion.1, s32[16]{0:T(128)S(1)} %get-tuple-element.14, f32[16,128,256]{2,1,0:T(8,128)} %copy.24), kind=kCustom, calls=%fused_computation.6 | custom fusion | flops 524288 | bytes 6291520 | tf_op jit(solution)/shard_map/scatter-add | solution.py:38
  105.9 4.4 %scatter_fusion.3 = f32[32,128,256]{2,1,0:T(8,128)} fusion(f32[32,128,256]{2,1,0:T(8,128)} %scatter_fusion.2, s32[16]{0:T(128)S(1)} %get-tuple-element.11, f32[16,128,256]{2,1,0:T(8,128)S(1)} %copy.25), kind=kCustom, calls=%fused_computation.7 | custom fusion | flops 524288 | bytes 6291520 | tf_op jit(solution)/shard_map/scatter-add | solution.py:38
  110.3 4.7 %fusion.23 = (f32[16,128,256]{2,1,0:T(8,128)}, f32[16,128,256]{2,1,0:T(8,128)}) fusion(f32[32,128,256]{2,1,0:T(8,128)} %scatter_fusion.3), kind=kLoop, calls=%fused_computation.50 | loop fusion | bytes 8388608 | tf_op jit(solution)/shard_map/slice | solution.py:40
  115.0 0.7 reduce-scatter.3.cloned.1.call-update
  115.7 29.9 %reduce-scatter.5.cloned.1.call-done = f32[512,256]{1,0:T(8,128)} async-done(((f32[2048,256]{1,0:T(8,128)}), f32[512,256]{1,0:T(8,128)}) %reduce-scatter.5.cloned.1.call-update) | async-done | bytes 524304 | tf_op jit(solution)/shard_map/reduce_scatter | solution.py:43
  145.5 3.4 %collective-permute-start.1 = (f32[512,256]{1,0:T(8,128)}, f32[512,256]{1,0:T(8,128)S(1)}, u32[]{:S(2)}, u32[]{:S(2)}) collective-permute-start(f32[512,256]{1,0:T(8,128)} %reduce-scatter.5.cloned.1.call-done), channel_id=1, source_target_pairs={{0,4},{4,8},{8,12},{1,5},{5,9},{9,13},{2,6},{6,10},{10,14},{3,7},{... | collective-permute-start | bytes 1572872 | tf_op jit(solution)/shard_map/ppermute | solution.py:10
  149.0 30.3 %reduce-scatter.3.cloned.1.call-done = f32[512,256]{1,0:T(8,128)} async-done(((f32[2048,256]{1,0:T(8,128)}), f32[512,256]{1,0:T(8,128)}) %reduce-scatter.3.cloned.1.call-update) | async-done | bytes 524304 | tf_op jit(solution)/shard_map/reduce_scatter | solution.py:42
  179.2 1.9 %add.57 = f32[512,256]{1,0:T(8,128)} add(f32[512,256]{1,0:T(8,128)} %reduce-scatter.3.cloned.1.call-done, f32[512,256]{1,0:T(8,128)S(1)} %collective-permute-done.1) | non-fusion elementwise | flops 131072 | bytes 1572864 | tf_op jit(solution)/shard_map/add | solution.py:45
  (18 shorter events, 1.2 us)
Async XLA Ops:
  6.5 21.8 %all-gather.2.cloned.1.call-start = ((), (), s32[]{:S(2)}) async-start(), calls=%async_computation.2 | async-start | bytes 1310720 | tf_op jit(solution)/shard_map/all_gather | solution.py:18
  7.3 138.3 %reduce-scatter.5.cloned.1.call-start = ((), (), s32[]{:S(2)}) async-start(), calls=%async_computation.4 | async-start | bytes 2621440 | tf_op jit(solution)/shard_map/reduce_scatter | solution.py:43
  28.3 27.4 %collective-permute-start = (bf16[2048,256]{1,0:T(8,128)(2,1)}, bf16[2048,256]{1,0:T(8,128)(2,1)S(1)}, u32[]{:S(2)}, u32[]{:S(2)}) collective-permute-start(bf16[2048,256]{1,0:T(8,128)(2,1)} %all-gather.2.cloned.1.call-done), channel_id=1, source_target_pairs={{4,0},{8,4},{12,8},{5,1},{9,5},{13,9},{6,2},{10,6},{14,10},{7,3},{... | collective-permute-start | bytes 3145736 | tf_op jit(solution)/shard_map/ppermute | solution.py:10
  59.3 3.0 %copy-start.2 = (bf16[16,128,256]{2,1,0:T(8,128)(2,1)S(1)}, bf16[16,128,256]{2,1,0:T(8,128)(2,1)}, u32[]{:S(2)}) copy-start(bf16[16,128,256]{2,1,0:T(8,128)(2,1)} %gather_fusion.1) | copy-start | bytes 3145732
  65.8 3.5 %copy-start.3 = (f32[16,128]{1,0:T(8,128)S(1)}, f32[16,128]{1,0:T(8,128)}, u32[]{:S(2)}) copy-start(f32[16,128]{1,0:T(8,128)} %param.9) | copy-start | bytes 24580
  69.2 4.2 %copy-start = (bf16[16,4,128,128]{3,2,1,0:T(8,128)(2,1)S(1)}, bf16[16,4,128,128]{3,2,1,0:T(8,128)(2,1)}, u32[]{:S(2)}) copy-start(bf16[16,4,128,128]{3,2,1,0:T(8,128)(2,1)} %param.6) | copy-start | bytes 6291460
  81.0 3.1 %copy-start.1 = (f32[16,128,256]{1,2,0:T(8,128)S(1)}, f32[16,128,256]{1,2,0:T(8,128)}, u32[]{:S(2)}) copy-start(f32[16,128,256]{1,2,0:T(8,128)} %multiply_bitcast_fusion.1) | copy-start | bytes 6291460
  114.9 64.3 %reduce-scatter.3.cloned.1.call-start = ((), (), s32[]{:S(2)}) async-start(), calls=%async_computation.3 | async-start | bytes 2621440 | tf_op jit(solution)/shard_map/reduce_scatter | solution.py:42
  145.5 33.7 %collective-permute-start.1 = (f32[512,256]{1,0:T(8,128)}, f32[512,256]{1,0:T(8,128)S(1)}, u32[]{:S(2)}, u32[]{:S(2)}) collective-permute-start(f32[512,256]{1,0:T(8,128)} %reduce-scatter.5.cloned.1.call-done), channel_id=1, source_target_pairs={{0,4},{4,8},{8,12},{1,5},{5,9},{9,13},{2,6},{6,10},{10,14},{3,7},{... | collective-permute-start | bytes 1572872 | tf_op jit(solution)/shard_map/ppermute | solution.py:10
Sparse Core Ops, SparseCore 0:
  8.9 19.4 all-gather.1
  115.0 30.4 reduce-scatter.4
  148.1 31.1 reduce-scatter.2
where the time goes:
time: 188 us
  waiting for transfers between devices  107 us (57%)
  other arithmetic  24.8 us (13%)
  local copies, waits for them, and re-layouts  19.2 us (10%)
  matrix products  18.5 us (10%)
  between operations  13.2 us (7%)
  starting transfers between devices  4.78 us (3%)
    reduce_scatter x1, waiting for transfers between devices, local(): lax.psum_scatter(own_part, 'vox', scatter_dimension=0, tiled=True)  30.3 us
    reduce_scatter x1, waiting for transfers between devices, local(): lax.psum_scatter(next_part, 'vox', scatter_dimension=0, tiled=True)  29.9 us
    ppermute x2, waiting for transfers between devices, shifted(): return lax.ppermute(array, axis, pairs)  24.5 us
    all_gather x1, waiting for transfers between devices, local(): own_panel = lax.all_gather(probes, 'vox', axis=0, tiled=True)  21 us
    scatter-add x4, other arithmetic, local(): partial_value.at[pattern[:, slot]].add(back * scales[:, slot, None, None])  20 us
    dot_general x4, matrix products, local(): jnp.einsum('rab,rbk->rak', blocks[:, slot], picked, preferred_element_typ...  12.8 us
    mul x4, local copies, waits for them, and re-layouts, local(): back * scales[:, slot, None, None]  8.68 us
    dot_general x4, matrix products, local(): jnp.einsum('rab,rak->rbk', blocks[:, slot], weighted, preferred_element_t...  5.68 us
  transfers between devices with their start and end apart: 5, of which 4 were waited for; matrix products, arithmetic and copies ran while one was open for 1% of the time, Pallas kernels for 0%

commit v1 on v0

v1 whole, which is shorter than its diff:
```python
import functools

import jax
import jax.numpy as jnp
from jax import lax
from jax.experimental import pallas as pl
from jax.experimental.pallas import tpu as pltpu
from jax.sharding import PartitionSpec as P

AXES = ("cohort", "grp", "vox")
CODE_BITS = 14


def core_swap(array):
    devices = lax.axis_size("vox")
    return lax.ppermute(array, "vox", [(i, i ^ 1) for i in range(devices)])


def hop(array, group_by, chip_by):
    groups, devices = lax.axis_size("grp"), lax.axis_size("vox")
    chips = devices // 2
    pairs = []
    for g in range(groups):
        for y in range(chips):
            for c in range(2):
                to = g + group_by
                if 0 <= to < groups:
                    target = 2 * ((y + chip_by) % chips) + c
                    pairs.append((g * devices + 2 * y + c, to * devices + target))
    return lax.ppermute(array, ("grp", "vox"), pairs)


def prepare_kernel(scale_ref, blocks_ref, wide_ref, tall_ref):
    rows, count, width, _ = blocks_ref.shape
    first = pl.program_id(0) * rows
    for r in range(rows):
        for n in range(count):
            scale = scale_ref[(first + r) * count + n]
            block = (blocks_ref[r, n].astype(jnp.float32) * scale).astype(jnp.bfloat16)
            wide_ref[r, :, n * width:(n + 1) * width] = block
            tall_ref[r, n * width:(n + 1) * width, :] = block.T


def prepare(scales, blocks):
    rows, count, width, _ = blocks.shape
    step = 4
    return pl.pallas_call(
        prepare_kernel,
        grid_spec=pltpu.PrefetchScalarGridSpec(
            num_scalar_prefetch=1,
            grid=(rows // step,),
            in_specs=[pl.BlockSpec((step, count, width, width), lambda i, s: (i, 0, 0, 0))],
            out_specs=[
                pl.BlockSpec((step, width, count * width), lambda i, s: (i, 0, 0)),
                pl.BlockSpec((step, count * width, width), lambda i, s: (i, 0, 0)),
            ],
        ),
        out_shape=[
            jax.ShapeDtypeStruct((rows, width, count * width), jnp.bfloat16),
            jax.ShapeDtypeStruct((rows, count * width, width), jnp.bfloat16),
        ],
        name="prepare",
        cost_estimate=pl.CostEstimate(flops=0, transcendentals=0, bytes_accessed=3 * blocks.size * 2),
    )(scales, blocks)


def apply_kernel(shards, pick_ref, put_ref, wide_ref, tall_ref, noise_ref, *refs):
    shard_refs = refs[:shards]
    sib_ref, keep_ref, panels, total, in_sem, out_sem = refs[shards:]
    rows, width, deep = wide_ref.shape
    count = deep // width
    per = shard_refs[0].shape[0] // width
    cols = noise_ref.shape[2]
    copies = [
        pltpu.make_async_copy(ref, panels.at[pl.ds(i * per * width, per * width)], in_sem.at[i])
        for i, ref in enumerate(shard_refs)
    ]
    for copy in copies:
        copy.start()
    total[...] = jnp.zeros_like(total)
    for copy in copies:
        copy.wait()

    def row(r, carry):
        picked = jnp.concatenate(
            [
                panels[pl.ds(pl.multiple_of(pick_ref[r * count + n] * width, width), width), :]
                for n in range(count)
            ],
            axis=0,
        )
        forward = jnp.dot(wide_ref[r], picked, preferred_element_type=jnp.float32)
        weight = noise_ref[r]
        parts = [weight * forward[:, k:k + cols] for k in range(0, forward.shape[1], cols)]
        weighted = jnp.concatenate(parts, axis=1).astype(jnp.bfloat16)
        back = jnp.dot(tall_ref[r], weighted, preferred_element_type=jnp.float32)
        for n in range(count):
            spot = pl.ds(pl.multiple_of(put_ref[r * count + n] * width, width), width)
            total[spot, :] += back[n * width:(n + 1) * width, :]
        return carry

    lax.fori_loop(0, rows, row, 0)
    half = total.shape[0] // 2
    outs = [
        pltpu.make_async_copy(total.at[pl.ds(0, half)], sib_ref, out_sem.at[0]),
        pltpu.make_async_copy(total.at[pl.ds(half, half)], keep_ref, out_sem.at[1]),
    ]
    for copy in outs:
        copy.start()
    for copy in outs:
        copy.wait()


def apply(pick, put, wide, tall, noise, shards):
    rows, width, deep = wide.shape
    cols = shards[0].shape[1]
    held = sum(s.shape[0] for s in shards)
    whole = pl.BlockSpec(memory_space=pltpu.VMEM)
    part = jax.ShapeDtypeStruct((held // 2, cols), jnp.float32)
    return pl.pallas_call(
        functools.partial(apply_kernel, len(shards)),
        grid_spec=pltpu.PrefetchScalarGridSpec(
            num_scalar_prefetch=2,
            grid=(),
            in_specs=[whole, whole, whole] + [pl.BlockSpec(memory_space=pl.ANY)] * len(shards),
            out_specs=[pl.BlockSpec(memory_space=pl.ANY)] * 2,
            scratch_shapes=[
                pltpu.VMEM((held, cols), jnp.bfloat16),
                pltpu.VMEM((held, cols), jnp.float32),
                pltpu.SemaphoreType.DMA((len(shards),)),
                pltpu.SemaphoreType.DMA((2,)),
            ],
        ),
        out_shape=[part, part],
        name="apply",
        cost_estimate=pl.CostEstimate(
            flops=4 * rows * width * deep * cols, transcendentals=0, bytes_accessed=4 * held * cols
        ),
    )(pick, put, wide, tall, noise, *shards)


def code_kernel(keep_ref, got_ref, own_ref, *code_refs):
    size = own_ref.shape[0]
    own_ref[...] = keep_ref[:size, :] + got_ref[:size, :]
    for i, code_ref in enumerate(code_refs):
        rows = slice((i + 1) * size, (i + 2) * size)
        value = keep_ref[rows, :] + got_ref[rows, :]
        most = jnp.max(jnp.abs(value), axis=0, keepdims=True)
        power = jnp.floor(jnp.log2(jnp.maximum(most, 1e-30))) + 1.0
        steps = jnp.round(value * jnp.exp2(CODE_BITS - power))
        code_ref[:size, :] = steps.astype(jnp.int32).astype(jnp.int16)
        mark = jnp.broadcast_to(power, (code_ref.shape[0] - size, power.shape[1]))
        code_ref[size:, :] = mark.astype(jnp.int32).astype(jnp.int16)


def code(keep, got, messages):
    size, cols = keep.shape[0] // (messages + 1), keep.shape[1]
    whole = pl.BlockSpec(memory_space=pltpu.VMEM)
    return pl.pallas_call(
        code_kernel,
        in_specs=[whole, whole],
        out_specs=[whole] * (messages + 1),
        out_shape=[jax.ShapeDtypeStruct((size, cols), jnp.float32)]
        + [jax.ShapeDtypeStruct((size + 16, cols), jnp.int16)] * messages,
        name="code",
        cost_estimate=pl.CostEstimate(flops=0, transcendentals=0, bytes_accessed=keep.size * 12),
    )(keep, got)


def join_kernel(own_ref, *refs):
    out_ref = refs[-1]
    size = own_ref.shape[0]
    value = own_ref[...]
    for code_ref in refs[:-1]:
        power = code_ref[size:, :].astype(jnp.int32).astype(jnp.float32)[:1, :]
        steps = code_ref[:size, :].astype(jnp.int32).astype(jnp.float32)
        value = value + steps * jnp.exp2(power - CODE_BITS)
    out_ref[...] = value


def join(own, codes):
    whole = pl.BlockSpec(memory_space=pltpu.VMEM)
    return pl.pallas_call(
        join_kernel,
        in_specs=[whole] * (1 + len(codes)),
        out_specs=whole,
        out_shape=jax.ShapeDtypeStruct(own.shape, jnp.float32),
        name="join",
        cost_estimate=pl.CostEstimate(flops=0, transcendentals=0, bytes_accessed=own.size * 14),
    )(own, *codes)


def local(probes, blocks, pattern, scale_exp, noise):
    rows_here, count, width, _ = blocks.shape
    chips = lax.axis_size("vox") // 2
    per = probes.shape[0] // width
    group = per * 2 * chips
    me = lax.axis_index("vox")
    chip, core = me // 2, me % 2

    far = [hop(probes, -1, -d) for d in range(1, chips)]
    near = [hop(probes, 0, -d) for d in range(1, chips)]
    ahead = hop(probes, -1, 0)
    mine = [probes] + near + [ahead] + far
    shards = []
    for shard in mine:
        shards += [shard, core_swap(shard)]

    column = pattern.reshape(-1)
    is_next = (column >= group).astype(jnp.int32)
    inside = column - is_next * group
    owner = inside // per
    distance = (owner // 2 - chip) % chips
    other = (owner % 2) ^ core
    within = inside % per
    pick = ((is_next * chips + distance) * 2 + other) * per + within
    put = ((1 - other) * 2 * chips + is_next * chips + distance) * per + within
    scales = jnp.exp2(scale_exp.reshape(-1).astype(jnp.float32))
    wide, tall = prepare(scales, blocks)
    weight = jnp.broadcast_to(noise[:, :, None], (rows_here, width, 128))

    sib, keep = apply(pick, put, wide, tall, weight, shards)
    got = core_swap(sib)
    own, *codes = code(keep, got, 2 * chips - 1)
    sent = []
    for i, value in enumerate(codes, start=1):
        sent.append(hop(value, i // chips, i % chips))
    return join(own, sent)


def solution(mesh):
    in_specs = (
        P(AXES, None),
        P(AXES, None, None, None),
        P(AXES, None),
        P(AXES, None),
        P(AXES, None),
    )
    out_specs = P(AXES, None)
    return jax.shard_map(local, mesh=mesh, in_specs=in_specs, out_specs=out_specs, check_vma=False)
```

time: 188 us -> 70.1 us (0.37)
  waiting for transfers between devices: 107 us -> 22.5 us
  Pallas kernels: 0 us -> 24.9 us
  other arithmetic: 24.8 us -> 1.92 us
  matrix products: 18.5 us -> 0 us
  local copies, waits for them, and re-layouts: 19.2 us -> 4.99 us
  between operations: 13.2 us -> 0.18 us
  starting transfers between devices: 4.78 us -> 15.2 us
    reduce_scatter x2 -> x0, waiting for transfers between devices: 60.2 us -> none  [the longest x1 30.3 us: local(): lax.psum_scatter(own_part, 'vox', scatter_dimension=0, tiled=True)]
    pallas_call x0 -> x4, Pallas kernels: none -> 24.9 us  [the longest x1 14 us: apply(): pl.pallas_call(functools.partial(apply_kernel, len(shards)), grid_spec=pl...]
    all_gather x1 -> x0, waiting for transfers between devices: 21 us -> none  [local(): own_panel = lax.all_gather(probes, 'vox', axis=0, tiled=True)]
    scatter-add x4 -> x0, other arithmetic: 20 us -> none  [local(): partial_value.at[pattern[:, slot]].add(back * scales[:, slot, None, None])]
    dot_general x8 -> x0, matrix products: 18.5 us -> none  [the longest x4 12.8 us: local(): jnp.einsum('rab,rbk->rak', blocks[:, slot], picked, preferred_element_typ...]
    ppermute x2 -> x11, starting transfers between devices: 4.7 us -> 15.2 us  [the longest x6 14.2 us: hop(): return lax.ppermute(array, ('grp', 'vox'), pairs)]
    mul x5 -> x0, local copies, waits for them, and re-layouts: 8.68 us -> none  [the longest x4 8.68 us: local(): back * scales[:, slot, None, None]]
    slice x1 -> x0, local copies, waits for them, and re-layouts: 4.65 us -> none  [local(): partial_value[group_rows:].reshape(group_rows * width, probe_cols)]
  transfers between devices with their start and end apart: 5 -> 11, of which waited for: 4 -> 6; matrix products, arithmetic and copies ran while one was open for 1% -> 5% of each run, Pallas kernels for 0% -> 7%
where the time goes in v1:
time: 70.1 us; the launch traced here: 69.7 us
  Pallas kernels  24.9 us (36%)
  waiting for transfers between devices  22.5 us (32%)
  starting transfers between devices  15.2 us (22%)
  local copies, waits for them, and re-layouts  4.99 us (7%)
  other arithmetic  1.92 us (3%)
    ppermute x6, waiting for transfers between devices, hop(): return lax.ppermute(array, ('grp', 'vox'), pairs)  18.5 us
    ppermute x6, starting transfers between devices, hop(): return lax.ppermute(array, ('grp', 'vox'), pairs)  14.2 us
    pallas_call x1, Pallas kernels, apply(): pl.pallas_call(functools.partial(apply_kernel, len(shards)), grid_spec=pl...  14 us
    pallas_call x1, Pallas kernels, prepare(): pl.pallas_call(prepare_kernel, grid_spec=pltpu.PrefetchScalarGridSpec(num...  5.07 us
    ppermute x5, waiting for transfers between devices, core_swap(): return lax.ppermute(array, 'vox', [(i, i ^ 1) for i in range(devices)])  4.01 us
    pallas_call x1, Pallas kernels, code(): pl.pallas_call(code_kernel, in_specs=[whole, whole], out_specs=[whole] *...  3.47 us
    unnamed x25, local copies, waits for them, and re-layouts  2.82 us
    pallas_call x1, Pallas kernels, join(): pl.pallas_call(join_kernel, in_specs=[whole] * (1 + len(codes)), out_spec...  2.28 us
  transfers between devices with their start and end apart: 11, of which 6 were waited for; matrix products, arithmetic and copies ran while one was open for 5% of the time, Pallas kernels for 7%

profile of v1, /device:TPU:0, one launch (start us, length us, event | category | flops | bytes accessed | tf_op | source)
XLA Modules:
  0.0 69.7 jit_solution(5391650247010991667)
XLA Ops:
  0.0 1.4 %collective-permute-start.3 = (bf16[512,256]{1,0:T(8,128)(2,1)}, bf16[512,256]{1,0:T(8,128)(2,1)S(1)}, u32[]{:S(2)}, u32[]{:S(2)}) collective-permute-start(bf16[512,256]{1,0:T(8,128)(2,1)} %refs_0_.1), channel_id=1, source_target_pairs={{4,0},{5,1},{6,2},{7,3},{8,4},{9,5},{10,6},{11,7},{12,8},{13,9},{1... | collective-permute-start | bytes 786440 | tf_op jit(solution)/shard_map/ppermute | solution.py:30
  1.4 3.1 %collective-permute-start.1 = (bf16[512,256]{1,0:T(8,128)(2,1)}, bf16[512,256]{1,0:T(8,128)(2,1)S(1)}, u32[]{:S(2)}, u32[]{:S(2)}) collective-permute-start(bf16[512,256]{1,0:T(8,128)(2,1)} %refs_0_.1), channel_id=1, source_target_pairs={{0,2},{1,3},{2,0},{3,1},{4,6},{5,7},{6,4},{7,5},{8,10},{9,11},{10,... | collective-permute-start | bytes 786440 | tf_op jit(solution)/shard_map/ppermute | solution.py:30
  4.5 0.0 collective-permute-start
  4.5 1.3 %collective-permute-start.5 = (bf16[512,256]{1,0:T(8,128)(2,1)}, bf16[512,256]{1,0:T(8,128)(2,1)S(1)}, u32[]{:S(2)}, u32[]{:S(2)}) collective-permute-start(bf16[512,256]{1,0:T(8,128)(2,1)} %refs_0_.1), channel_id=1, source_target_pairs={{4,2},{5,3},{6,0},{7,1},{8,6},{9,7},{10,4},{11,5},{12,10},{13,11},... | collective-permute-start | bytes 786440 | tf_op jit(solution)/shard_map/ppermute | solution.py:30
  5.8 0.8 %copy.8 = s32[16,4]{1,0:T(8,128)S(1)} copy(s32[16,4]{0,1:T(4,128)} %param.7) | data formatting | bytes 512 | tf_op args[2]
  6.5 0.1 reshape.9
  6.7 0.7 multiply_exponential_fusion
  7.3 5.1 %collective-permute-done.3.refs_4_ = bf16[512,256]{1,0:T(8,128)(2,1)S(1)} collective-permute-done((bf16[512,256]{1,0:T(8,128)(2,1)}, bf16[512,256]{1,0:T(8,128)(2,1)S(1)}, u32[]{:S(2)}, u32[]{:S(2)}) %collective-permute-start.3) | collective-permute-done | bytes 262176 | tf_op jit(solution)/shard_map/ppermute | solution.py:30
  12.4 0.0 collective-permute-start.4
  12.4 0.0 collective-permute-done.1.refs_2_
  12.5 0.5 collective-permute-start.2
  13.0 5.4 %collective-permute-done.5.refs_6_ = bf16[512,256]{1,0:T(8,128)(2,1)S(1)} collective-permute-done((bf16[512,256]{1,0:T(8,128)(2,1)}, bf16[512,256]{1,0:T(8,128)(2,1)S(1)}, u32[]{:S(2)}, u32[]{:S(2)}) %collective-permute-start.5) | collective-permute-done | bytes 262176 | tf_op jit(solution)/shard_map/ppermute | solution.py:30
  18.3 0.0 collective-permute-start.6
  18.3 0.6 multiply_add_fusion
  19.0 0.1 copy.9
  19.0 0.6 exp2.15.scale_ref
  19.6 5.1 %prepare.1 = (bf16[16,128,512]{2,1,0:T(8,128)(2,1)}, bf16[16,512,128]{2,1,0:T(8,128)(2,1)}) custom-call(f32[64]{0:T(128)} %exp2.15.scale_ref, bf16[16,4,128,128]{3,2,1,0:T(8,128)(2,1)} %blocks_ref.1), custom_call_target="tpu_custom_call" | custom-call | bytes 6291456 | tf_op jit(solution)/shard_map/prepare/pallas_call | solution.py:47
  24.7 0.6 multiply_add_fusion.1.pick_ref
  25.4 1.4 %broadcast_in_dim.2.noise_ref = f32[16,128,128]{2,1,0:T(8,128)} broadcast(f32[16,128]{1,0:T(8,128)S(1)} %copy-done.11), dimensions={0,1} | broadcast | bytes 1056768 | tf_op jit(solution)/shard_map/broadcast_in_dim | solution.py:220
  26.8 14.0 %apply.1 = (f32[2048,256]{1,0:T(8,128)}, f32[2048,256]{1,0:T(8,128)}) custom-call(s32[64]{0:T(128)} %multiply_add_fusion.1.pick_ref, s32[64]{0:T(128)} %get-tuple-element.21.put_ref, bf16[16,128,512]{2,1,0:T(8,128)(2,1)} %get-tuple-element.13.wide_ref, bf16[16,512,128]{2,1,0:T(8,128)(2,1)} %get-tuple-element.14.tall_ref, ...), custom_call_target="tpu_custom_call" | custom-call | flops 1073741824 | bytes 4194304 | tf_op jit(solution)/shard_map/apply/pallas_call | solution.py:120
  40.9 0.5 collective-permute-start.7
  41.4 4.0 %collective-permute-done.7.got_ref = f32[2048,256]{1,0:T(8,128)S(1)} collective-permute-done((f32[2048,256]{1,0:T(8,128)}, f32[2048,256]{1,0:T(8,128)S(1)}, u32[]{:S(2)}, u32[]{:S(2)}) %collective-permute-start.7) | collective-permute-done | bytes 2097184 | tf_op jit(solution)/shard_map/ppermute | solution.py:16
  45.4 1.3 %copy-done = f32[2048,256]{1,0:T(8,128)} copy-done((f32[2048,256]{1,0:T(8,128)}, f32[2048,256]{1,0:T(8,128)S(1)}, u32[]{:S(2)}) %copy-start) | copy-done | bytes 2097176
  46.7 3.5 %code.1 = (f32[512,256]{1,0:T(8,128)}, s16[528,256]{1,0:T(8,128)(2,1)}, s16[528,256]{1,0:T(8,128)(2,1)}, s16[528,256]{1,0:T(8,128)(2,1)}) custom-call(f32[2048,256]{1,0:T(8,128)} %get-tuple-element.15.keep_ref, f32[2048,256]{1,0:T(8,128)} %copy-done), custom_call_target="tpu_custom_call" | custom-call | bytes 6291456 | tf_op jit(solution)/shard_map/code/pallas_call | solution.py:159
  50.2 0.3 collective-permute-start.8
  50.5 4.3 %collective-permute-start.9 = (s16[528,256]{1,0:T(8,128)(2,1)}, s16[528,256]{1,0:T(8,128)(2,1)S(1)}, u32[]{:S(2)}, u32[]{:S(2)}) collective-permute-start(s16[528,256]{1,0:T(8,128)(2,1)} %get-tuple-element.19), channel_id=1, source_target_pairs={{0,4},{1,5},{2,6},{3,7},{4,8},{5,9},{6,10},{7,11},{8,12},{9,13},{1... | collective-permute-start | bytes 811016 | tf_op jit(solution)/shard_map/ppermute | solution.py:30
  54.9 3.7 %collective-permute-start.10 = (s16[528,256]{1,0:T(8,128)(2,1)}, s16[528,256]{1,0:T(8,128)(2,1)S(1)}, u32[]{:S(2)}, u32[]{:S(2)}) collective-permute-start(s16[528,256]{1,0:T(8,128)(2,1)} %get-tuple-element.20), channel_id=1, source_target_pairs={{0,6},{1,7},{2,4},{3,5},{4,10},{5,11},{6,8},{7,9},{8,14},{9,15},{1... | collective-permute-start | bytes 811016 | tf_op jit(solution)/shard_map/ppermute | solution.py:30
  58.6 0.5 collective-permute-done.8.refs_0_
  59.1 2.9 %collective-permute-done.9.refs_1_ = s16[528,256]{1,0:T(8,128)(2,1)S(1)} collective-permute-done((s16[528,256]{1,0:T(8,128)(2,1)}, s16[528,256]{1,0:T(8,128)(2,1)S(1)}, u32[]{:S(2)}, u32[]{:S(2)}) %collective-permute-start.9) | collective-permute-done | bytes 270368 | tf_op jit(solution)/shard_map/ppermute | solution.py:30
  62.0 4.7 %collective-permute-done.10.refs_2_ = s16[528,256]{1,0:T(8,128)(2,1)S(1)} collective-permute-done((s16[528,256]{1,0:T(8,128)(2,1)}, s16[528,256]{1,0:T(8,128)(2,1)S(1)}, u32[]{:S(2)}, u32[]{:S(2)}) %collective-permute-start.10) | collective-permute-done | bytes 270368 | tf_op jit(solution)/shard_map/ppermute | solution.py:30
  66.7 0.7 %copy-done.3 = s16[528,256]{1,0:T(8,128)(2,1)} copy-done((s16[528,256]{1,0:T(8,128)(2,1)}, s16[528,256]{1,0:T(8,128)(2,1)S(1)}, u32[]{:S(2)}) %copy-start.3) | copy-done | bytes 270360
  67.4 2.3 %join.1 = f32[512,256]{1,0:T(8,128)} custom-call(f32[512,256]{1,0:T(8,128)} %get-tuple-element.17.own_ref, s16[528,256]{1,0:T(8,128)(2,1)} %copy-done.1, s16[528,256]{1,0:T(8,128)(2,1)} %copy-done.2, s16[528,256]{1,0:T(8,128)(2,1)} %copy-done.3), custom_call_target="tpu_custom_call" | custom-call | bytes 1835008 | tf_op jit(solution)/shard_map/join/pallas_call | solution.py:183
  (27 shorter events, 0.1 us)
Async XLA Ops:
  0.0 25.4 %copy-start.11 = (f32[16,128]{1,0:T(8,128)S(1)}, f32[16,128]{1,0:T(8,128)}, u32[]{:S(2)}) copy-start(f32[16,128]{1,0:T(8,128)} %param.9) | copy-start | bytes 24580
  0.0 12.4 %collective-permute-start.3 = (bf16[512,256]{1,0:T(8,128)(2,1)}, bf16[512,256]{1,0:T(8,128)(2,1)S(1)}, u32[]{:S(2)}, u32[]{:S(2)}) collective-permute-start(bf16[512,256]{1,0:T(8,128)(2,1)} %refs_0_.1), channel_id=1, source_target_pairs={{4,0},{5,1},{6,2},{7,3},{8,4},{9,5},{10,6},{11,7},{12,8},{13,9},{1... | collective-permute-start | bytes 786440 | tf_op jit(solution)/shard_map/ppermute | solution.py:30
  1.4 11.0 %collective-permute-start.1 = (bf16[512,256]{1,0:T(8,128)(2,1)}, bf16[512,256]{1,0:T(8,128)(2,1)S(1)}, u32[]{:S(2)}, u32[]{:S(2)}) collective-permute-start(bf16[512,256]{1,0:T(8,128)(2,1)} %refs_0_.1), channel_id=1, source_target_pairs={{0,2},{1,3},{2,0},{3,1},{4,6},{5,7},{6,4},{7,5},{8,10},{9,11},{10,... | collective-permute-start | bytes 786440 | tf_op jit(solution)/shard_map/ppermute | solution.py:30
  4.5 20.8 %collective-permute-start = (bf16[512,256]{1,0:T(8,128)(2,1)}, bf16[512,256]{1,0:T(8,128)(2,1)S(1)}, u32[]{:S(2)}, u32[]{:S(2)}) collective-permute-start(bf16[512,256]{1,0:T(8,128)(2,1)} %refs_0_.1), channel_id=1, source_target_pairs={{0,1},{1,0},{2,3},{3,2},{4,5},{5,4},{6,7},{7,6},{8,9},{9,8},{10,11... | collective-permute-start | bytes 786440 | tf_op jit(solution)/shard_map/ppermute | solution.py:16
  4.5 13.8 %collective-permute-start.5 = (bf16[512,256]{1,0:T(8,128)(2,1)}, bf16[512,256]{1,0:T(8,128)(2,1)S(1)}, u32[]{:S(2)}, u32[]{:S(2)}) collective-permute-start(bf16[512,256]{1,0:T(8,128)(2,1)} %refs_0_.1), channel_id=1, source_target_pairs={{4,2},{5,3},{6,0},{7,1},{8,6},{9,7},{10,4},{11,5},{12,10},{13,11},... | collective-permute-start | bytes 786440 | tf_op jit(solution)/shard_map/ppermute | solution.py:30
  12.4 14.3 %copy-start.4 = (bf16[512,256]{1,0:T(8,128)(2,1)}, bf16[512,256]{1,0:T(8,128)(2,1)S(1)}, u32[]{:S(2)}) copy-start(bf16[512,256]{1,0:T(8,128)(2,1)S(1)} %collective-permute-done.3.refs_4_) | copy-start | bytes 786436
  12.4 12.9 %collective-permute-start.4 = (bf16[512,256]{1,0:T(8,128)(2,1)S(1)}, bf16[512,256]{1,0:T(8,128)(2,1)S(1)}, u32[]{:S(2)}, u32[]{:S(2)}) collective-permute-start(bf16[512,256]{1,0:T(8,128)(2,1)S(1)} %collective-permute-done.3.refs_4_), channel_id=1, source_target_pairs={{0,1},{1,0},{2,3},{3,2},{4,5},{5,4},{6,7},{7,6},{8,9},{9,8},{10,11... | collective-permute-start | bytes 786440 | tf_op jit(solution)/shard_map/ppermute | solution.py:16
  12.5 14.3 %copy-start.5 = (bf16[512,256]{1,0:T(8,128)(2,1)}, bf16[512,256]{1,0:T(8,128)(2,1)S(1)}, u32[]{:S(2)}) copy-start(bf16[512,256]{1,0:T(8,128)(2,1)S(1)} %collective-permute-done.1.refs_2_) | copy-start | bytes 786436
  12.5 12.9 %collective-permute-start.2 = (bf16[512,256]{1,0:T(8,128)(2,1)S(1)}, bf16[512,256]{1,0:T(8,128)(2,1)S(1)}, u32[]{:S(2)}, u32[]{:S(2)}) collective-permute-start(bf16[512,256]{1,0:T(8,128)(2,1)S(1)} %collective-permute-done.1.refs_2_), channel_id=1, source_target_pairs={{0,1},{1,0},{2,3},{3,2},{4,5},{5,4},{6,7},{7,6},{8,9},{9,8},{10,11... | collective-permute-start | bytes 786440 | tf_op jit(solution)/shard_map/ppermute | solution.py:16
  18.3 8.5 %copy-start.7 = (bf16[512,256]{1,0:T(8,128)(2,1)}, bf16[512,256]{1,0:T(8,128)(2,1)S(1)}, u32[]{:S(2)}) copy-start(bf16[512,256]{1,0:T(8,128)(2,1)S(1)} %collective-permute-done.5.refs_6_) | copy-start | bytes 786436
  18.3 7.0 %collective-permute-start.6 = (bf16[512,256]{1,0:T(8,128)(2,1)S(1)}, bf16[512,256]{1,0:T(8,128)(2,1)S(1)}, u32[]{:S(2)}, u32[]{:S(2)}) collective-permute-start(bf16[512,256]{1,0:T(8,128)(2,1)S(1)} %collective-permute-done.5.refs_6_), channel_id=1, source_target_pairs={{0,1},{1,0},{2,3},{3,2},{4,5},{5,4},{6,7},{7,6},{8,9},{9,8},{10,11... | collective-permute-start | bytes 786440 | tf_op jit(solution)/shard_map/ppermute | solution.py:16
  25.3 1.5 %copy-start.6 = (bf16[512,256]{1,0:T(8,128)(2,1)}, bf16[512,256]{1,0:T(8,128)(2,1)S(1)}, u32[]{:S(2)}) copy-start(bf16[512,256]{1,0:T(8,128)(2,1)S(1)} %collective-permute-done.refs_1_) | copy-start | bytes 786436
  25.3 1.5 %copy-start.8 = (bf16[512,256]{1,0:T(8,128)(2,1)}, bf16[512,256]{1,0:T(8,128)(2,1)S(1)}, u32[]{:S(2)}) copy-start(bf16[512,256]{1,0:T(8,128)(2,1)S(1)} %collective-permute-done.4.refs_5_) | copy-start | bytes 786436
  25.3 1.5 %copy-start.9 = (bf16[512,256]{1,0:T(8,128)(2,1)}, bf16[512,256]{1,0:T(8,128)(2,1)S(1)}, u32[]{:S(2)}) copy-start(bf16[512,256]{1,0:T(8,128)(2,1)S(1)} %collective-permute-done.2.refs_3_) | copy-start | bytes 786436
  25.4 1.5 %copy-start.10 = (bf16[512,256]{1,0:T(8,128)(2,1)}, bf16[512,256]{1,0:T(8,128)(2,1)S(1)}, u32[]{:S(2)}) copy-start(bf16[512,256]{1,0:T(8,128)(2,1)S(1)} %collective-permute-done.6.refs_7_) | copy-start | bytes 786436
  40.9 4.5 %collective-permute-start.7 = (f32[2048,256]{1,0:T(8,128)}, f32[2048,256]{1,0:T(8,128)S(1)}, u32[]{:S(2)}, u32[]{:S(2)}) collective-permute-start(f32[2048,256]{1,0:T(8,128)} %get-tuple-element.16), channel_id=1, source_target_pairs={{0,1},{1,0},{2,3},{3,2},{4,5},{5,4},{6,7},{7,6},{8,9},{9,8},{10,11... | collective-permute-start | bytes 6291464 | tf_op jit(solution)/shard_map/ppermute | solution.py:16
  45.4 1.3 %copy-start = (f32[2048,256]{1,0:T(8,128)}, f32[2048,256]{1,0:T(8,128)S(1)}, u32[]{:S(2)}) copy-start(f32[2048,256]{1,0:T(8,128)S(1)} %collective-permute-done.7.got_ref) | copy-start | bytes 6291460
  50.2 9.0 %collective-permute-start.8 = (s16[528,256]{1,0:T(8,128)(2,1)}, s16[528,256]{1,0:T(8,128)(2,1)S(1)}, u32[]{:S(2)}, u32[]{:S(2)}) collective-permute-start(s16[528,256]{1,0:T(8,128)(2,1)} %get-tuple-element.18), channel_id=1, source_target_pairs={{0,2},{1,3},{2,0},{3,1},{4,6},{5,7},{6,4},{7,5},{8,10},{9,11},{10,... | collective-permute-start | bytes 811016 | tf_op jit(solution)/shard_map/ppermute | solution.py:30
  50.5 11.5 %collective-permute-start.9 = (s16[528,256]{1,0:T(8,128)(2,1)}, s16[528,256]{1,0:T(8,128)(2,1)S(1)}, u32[]{:S(2)}, u32[]{:S(2)}) collective-permute-start(s16[528,256]{1,0:T(8,128)(2,1)} %get-tuple-element.19), channel_id=1, source_target_pairs={{0,4},{1,5},{2,6},{3,7},{4,8},{5,9},{6,10},{7,11},{8,12},{9,13},{1... | collective-permute-start | bytes 811016 | tf_op jit(solution)/shard_map/ppermute | solution.py:30
  54.9 11.8 %collective-permute-start.10 = (s16[528,256]{1,0:T(8,128)(2,1)}, s16[528,256]{1,0:T(8,128)(2,1)S(1)}, u32[]{:S(2)}, u32[]{:S(2)}) collective-permute-start(s16[528,256]{1,0:T(8,128)(2,1)} %get-tuple-element.20), channel_id=1, source_target_pairs={{0,6},{1,7},{2,4},{3,5},{4,10},{5,11},{6,8},{7,9},{8,14},{9,15},{1... | collective-permute-start | bytes 811016 | tf_op jit(solution)/shard_map/ppermute | solution.py:30
  59.1 7.6 %copy-start.1 = (s16[528,256]{1,0:T(8,128)(2,1)}, s16[528,256]{1,0:T(8,128)(2,1)S(1)}, u32[]{:S(2)}) copy-start(s16[528,256]{1,0:T(8,128)(2,1)S(1)} %collective-permute-done.8.refs_0_) | copy-start | bytes 811012
  62.0 4.7 %copy-start.2 = (s16[528,256]{1,0:T(8,128)(2,1)}, s16[528,256]{1,0:T(8,128)(2,1)S(1)}, u32[]{:S(2)}) copy-start(s16[528,256]{1,0:T(8,128)(2,1)S(1)} %collective-permute-done.9.refs_1_) | copy-start | bytes 811012
  66.7 0.7 %copy-start.3 = (s16[528,256]{1,0:T(8,128)(2,1)}, s16[528,256]{1,0:T(8,128)(2,1)S(1)}, u32[]{:S(2)}) copy-start(s16[528,256]{1,0:T(8,128)(2,1)S(1)} %collective-permute-done.10.refs_2_) | copy-start | bytes 811012
